TPU v7x, 256 devices: a whole 4x4x8 slice. The times are simulated.
256 devices in a mesh: dp: 32 (over x_lo, z, core), expert: 8 (over x_hi, y).
Axes of the slice: x: 4 (x_hi: 2, x_lo: 2; x = x_hi * 2 + x_lo), y: 4, z: 8, core: 2. Of those that a mesh axis runs over, the one named last changes fastest.
Arguments:
- tokens: bfloat16 [49152, 4096], P(('dp', 'expert')), may hold values from -24 to 24
- routes: int32 [49152, 2], P(('dp', 'expert')), may hold values from 0 to 7, all different within a row; in each aligned block of 192 rows (0 to 191, 192 to 383, ...) at most 64 rows name the same one
- positives: int32 [512], P(('dp', 'expert')), may hold values from 0 to 511, each once
- expert_out: bfloat16 [32, 8, 8, 64, 4096], P('dp', 'expert'), may hold values from -6 to 6
- router: bfloat16 [4096, 8], replicated, may hold values from -0.09375 to 0.09375
- norm_gain: float32 [4096], replicated, may hold values from 0.25 to 1.75
- loss_scale: float32 [], replicated, may hold values from 8192 to 65536
Outputs:
- token_grad: bfloat16 [49152, 4096], P(('dp', 'expert'))
- expert_grad: bfloat16 [32, 8, 8, 64, 4096], P('dp', 'expert')
- router_grad: float32 [4096, 8], replicated
- loss: float32 [], replicated
Inputs may be any that keep to these rules, and one draw needn't show every extreme that they name: `routes`: each row names 2 different experts; among the rows of one device no expert is named by more than 64 rows, a bound that some block reaches. `positives`: A permutation of the records.
All inputs are finite; a program needn't handle non-finite values.
Results may differ from a plain program's by a relative error of at most 0.0061.
Values may be sent and summed in bfloat16 or wider, within the bound.
No kernel may reach another device: no remote copies, remote signals or barrier semaphores. Data moves between devices by JAX's collectives and lax.ppermute only.
A program may use at most 128 MiB of HBM per device.

v0:
```python
import math
import jax
import jax.numpy as jnp
from jax import lax
from jax.sharding import PartitionSpec as P

PAIR_DEV = 2
SEQ = 48
norm_eps = 1e-05


def slot_where(routes, experts, capacity):
    hit_table = (routes[:, :, None] == jnp.arange(experts, dtype=jnp.int32)[None, None, :]).astype(
        jnp.int32
    )
    flat_hits = hit_table.reshape(-1, experts)
    before = jnp.cumsum(flat_hits, axis=0) - flat_hits
    slot_rank = jnp.sum(before * flat_hits, axis=1).reshape(routes.shape)
    return routes * capacity + slot_rank


def forward_rows(tokens, routes, received, router, norm_gain):
    experts = received.shape[0]
    capacity = received.shape[1]
    hidden_width = received.shape[2]
    logits = jnp.dot(tokens, router, preferred_element_type=jnp.float32)
    one_hot = (routes[:, :, None] == jnp.arange(experts, dtype=jnp.int32)[None, None, :]).astype(
        jnp.float32
    )
    chosen = jnp.sum(one_hot * logits[:, None, :], axis=2)
    gate_mix = jax.nn.softmax(chosen, axis=1)
    slot_rows = slot_where(routes, experts, capacity)
    fetched = received.reshape(experts * capacity, hidden_width)[slot_rows]
    summed_rows = (
        tokens.astype(jnp.float32)
        + gate_mix[:, 0:1] * fetched[:, 0].astype(jnp.float32)
        + gate_mix[:, 1:2] * fetched[:, 1].astype(jnp.float32)
    )
    inverse = lax.rsqrt(jnp.mean(summed_rows * summed_rows, axis=1, keepdims=True) + norm_eps)
    normed = summed_rows * inverse * norm_gain
    pooled = jnp.mean(normed.reshape(-1, SEQ, hidden_width), axis=1).astype(jnp.bfloat16)
    return (pooled, (gate_mix, one_hot, slot_rows, fetched, summed_rows, inverse))


def backward_rows(tokens, router, norm_gain, saved, grad_pool, experts, capacity):
    gate_mix, one_hot, slot_rows, fetched, summed_rows, inverse = saved
    hidden_width = tokens.shape[1]
    grad_rows = jnp.broadcast_to(
        grad_pool[:, None, :] / SEQ, (grad_pool.shape[0], SEQ, hidden_width)
    ).reshape(-1, hidden_width)
    weighted = grad_rows * norm_gain
    grad_summed = inverse * weighted - summed_rows * inverse**3 * jnp.mean(
        weighted * summed_rows, axis=1, keepdims=True
    )
    grad_gate = jnp.sum(grad_summed[:, None, :] * fetched.astype(jnp.float32), axis=2)
    grad_chosen = gate_mix * (grad_gate - jnp.sum(gate_mix * grad_gate, axis=1, keepdims=True))
    grad_logits = jnp.sum(one_hot * grad_chosen[:, :, None], axis=1).astype(jnp.bfloat16)
    router_part = lax.dot_general(
        tokens, grad_logits, (((0,), (0,)), ((), ())), preferred_element_type=jnp.float32
    )
    through_router = lax.dot_general(
        grad_logits, router, (((1,), (1,)), ((), ())), preferred_element_type=jnp.float32
    )
    token_grad = (grad_summed + through_router).astype(jnp.bfloat16)
    outgoing = (
        (gate_mix[:, :, None] * grad_summed[:, None, :])
        .astype(jnp.bfloat16)
        .reshape(-1, hidden_width)
    )
    sendback = (
        jnp.zeros((experts * capacity, hidden_width), jnp.bfloat16)
        .at[slot_rows.reshape(-1)]
        .set(outgoing)
    )
    return (token_grad, sendback.reshape(experts, capacity, hidden_width), router_part)


def score_rows(queries, records_all, positives, loss_scale, pair_total, score_scale):
    scores = (
        lax.dot_general(
            queries, records_all, (((1,), (1,)), ((), ())), preferred_element_type=jnp.float32
        )
        * score_scale
    )
    highest = jnp.max(scores, axis=1, keepdims=True)
    log_total = highest[:, 0] + jnp.log(jnp.sum(jnp.exp(scores - highest), axis=1))
    is_positive = jnp.arange(pair_total, dtype=jnp.int32)[None, :] == positives[:, None]
    positive_score = jnp.sum(jnp.where(is_positive, scores, jnp.zeros_like(scores)), axis=1)
    row_loss = log_total - positive_score
    softmax_rows = jnp.exp(scores - log_total[:, None])
    score_grad = (
        (softmax_rows - is_positive.astype(jnp.float32)) * (loss_scale / pair_total)
    ).astype(jnp.bfloat16)
    return (row_loss, score_grad)


def shards(tokens, routes, positives, expert_out, router, norm_gain, loss_scale):
    experts = expert_out.shape[2]
    capacity = expert_out.shape[3]
    hidden_width = expert_out.shape[4]
    received = lax.all_to_all(
        expert_out.reshape(experts, capacity, hidden_width),
        "expert",
        split_axis=0,
        concat_axis=0,
        tiled=True,
    )
    pooled, saved = forward_rows(tokens, routes, received, router, norm_gain)
    queries = pooled[:PAIR_DEV]
    records = pooled[PAIR_DEV:]
    loop_size = lax.axis_size("dp")
    column_size = lax.axis_size("expert")
    device_count = loop_size * column_size
    pair_total = PAIR_DEV * device_count
    score_scale = 4.0 / math.sqrt(hidden_width)
    records_all = lax.all_gather(records, ("dp", "expert"), axis=0, tiled=True)
    row_loss, score_grad = score_rows(
        queries, records_all, positives, loss_scale, pair_total, score_scale
    )
    loss_local = jnp.sum(row_loss)
    grad_queries = (
        jnp.dot(score_grad, records_all, preferred_element_type=jnp.float32) * score_scale
    )
    grad_records = lax.psum_scatter(
        lax.dot_general(
            score_grad, queries, (((0,), (0,)), ((), ())), preferred_element_type=jnp.float32
        )
        * score_scale,
        ("dp", "expert"),
        scatter_dimension=0,
        tiled=True,
    )
    grad_pool = jnp.concatenate([grad_queries, grad_records], axis=0)
    token_grad, sendback, router_part = backward_rows(
        tokens, router, norm_gain, saved, grad_pool, experts, capacity
    )
    returned = lax.all_to_all(sendback, "expert", split_axis=0, concat_axis=0, tiled=True)
    router_grad, loss_total = lax.psum((router_part, loss_local), ("dp", "expert"))
    expert_grad = returned.reshape(1, 1, experts, capacity, hidden_width)
    return (token_grad, expert_grad, router_grad, loss_total / pair_total)


def solution(mesh):
    placed = (
        P(("dp", "expert"), None),
        P(("dp", "expert"), None),
        P(("dp", "expert")),
        P("dp", "expert", None, None, None),
        P(),
        P(),
        P(),
    )
    return jax.shard_map(
        shards,
        mesh=mesh,
        in_specs=placed,
        out_specs=(P(("dp", "expert"), None), P("dp", "expert", None, None, None), P(), P()),
        check_vma=False,
    )
```

profile of v0, /device:TPU:8, one launch (start us, length us, event | category | flops | bytes accessed | tf_op | source)
XLA Modules:
  0.0 1506.5 jit_solution(1943185011051784695)
XLA Ops:
  7.2 7.5 all-to-all-start
  14.7 0.1 copy.45
  14.9 0.1 eq.59
  15.0 0.1 eq.55
  15.2 0.9 reduce-window.6
  16.0 0.2 slice_reduce_fusion
  16.4 0.1 reshape.211
  16.6 0.1 copy.48
  16.8 0.1 reshape.221
  16.9 0.5 fusion.20
  17.5 45.7 %all-to-all-done = bf16[8,64,4096]{2,1,0:T(8,128)(2,1)} async-done(((bf16[8,64,4096]{2,1,0:T(8,128)(2,1)}), bf16[8,64,4096]{2,1,0:T(8,128)(2,1)}, u32[]{:S(2)}, u32[]{:S(2)}) %all-to-all-start) | async-done | bytes 4194336 | tf_op jit(solution)/shard_map/all_to_all | solution.py:101
  63.2 11.0 gather_fusion
  74.2 4.6 reshape.220
  78.8 7.0 fusion.17
  85.8 4.0 multiply_reduce_fusion.2
  89.9 2.4 multiply_multiply_fusion
  92.3 0.2 copy-done.2
  92.5 2.2 reduce_sum.112
  94.7 0.6 slice_bitcast_fusion
  95.3 0.2 all-reduce.6.cloned.1.call-start
  96.2 680.8 %all-gather.3.cloned.1.call-done = bf16[256,2,4096]{2,1,0:T(2,128)(2,1)} async-done(((bf16[1,2,4096]{2,1,0:T(2,128)(2,1)}), bf16[256,2,4096]{2,1,0:T(2,128)(2,1)}) %all-gather.3.cloned.1.call-update) | async-done | bytes 4194320 | tf_op jit(solution)/shard_map/all_gather | solution.py:116
  777.0 7.2 reshape.238
  784.2 3.5 fusion.19
  787.7 0.2 select_reduce_fusion.2
  787.9 0.6 subtract_reduce_fusion
  788.5 4.6 convolution_multiply_fusion
  793.3 0.1 div.48
  793.4 0.1 copy.53
  793.5 0.1 reshape.214
  793.7 2.9 convolution_multiply_fusion.1
  796.6 301.1 %all-reduce.6.cloned.1.call-done = f32[512,4096]{1,0:T(8,128)} async-done(((f32[512,4096]{1,0:T(8,128)}), f32[512,4096]{1,0:T(8,128)}) %all-reduce.6.cloned.1.call-update) | async-done | bytes 8388624
  1097.7 1.1 constant_dynamic-slice_fusion
  1098.8 0.3 bitcast_multiply_fusion
  1099.2 0.5 copy-done.3
  1099.7 0.4 multiply_reduce_fusion.1
  1100.1 0.7 multiply_subtract_fusion
  1100.8 1.7 copy-done.1
  1102.5 5.3 mul.182
  1107.8 8.4 mul.189
  1116.2 9.7 scatter_custom_fusion
  1125.9 6.8 all-to-all-start.1
  1132.6 112.4 %psum.15 = f32[]{:T(128)} all-reduce(f32[]{:T(128)} %get-tuple-element.6), channel_id=1, replica_groups=mesh['dp'=32,'expert'=8] {'dp','expert'}, use_global_device_ids=true, to_apply=%region_19.20 | all-reduce | flops 1 | bytes 8 | tf_op jit(solution)/shard_map/psum | solution.py:138
  1245.7 5.7 multiply_reduce_fusion
  1251.5 2.4 convolution_bitcast_fusion
  1254.0 3.6 fusion
  1257.6 235.8 %all-reduce.4.cloned.1.call-done = f32[4096,8]{0,1:T(8,128)} async-done(((f32[4096,8]{0,1:T(8,128)}), f32[4096,8]{0,1:T(8,128)}) %all-reduce.4.cloned.1.call-update) | async-done | bytes 131088 | tf_op jit(solution)/shard_map/psum | solution.py:138
  1493.4 4.7 copy.69
  1498.2 0.7 copy.70
  (44 shorter events, 0.8 us)
Async XLA Ops:
  7.2 9.7 copy-start
  7.2 7.5 copy-start.8
  7.2 9.7 copy-start.4
  7.2 56.0 %all-to-all-start = ((bf16[8,64,4096]{2,1,0:T(8,128)(2,1)}), bf16[8,64,4096]{2,1,0:T(8,128)(2,1)}, u32[]{:S(2)}, u32[]{:S(2)}) async-start(bf16[8,64,4096]{2,1,0:T(8,128)(2,1)} %bitcast.46), calls=%async_computation | async-start | bytes 8388608 | tf_op jit(solution)/shard_map/all_to_all | solution.py:101
  14.7 762.3 %all-gather.3.cloned.1.call-start = ((), (), s32[]{:S(2)}) async-start(), calls=%async_computation.3 | async-start | bytes 4210688 | tf_op jit(solution)/shard_map/all_gather | solution.py:116
  78.8 7.0 copy-start.5
  85.8 4.1 copy-start.6
  89.8 2.6 copy-start.2
  95.3 1002.4 %all-reduce.6.cloned.1.call-start = ((), (), s32[]{:S(2)}) async-start(), calls=%async_computation.4 | async-start | bytes 16777216
  784.2 3.5 copy-start.9
  1097.7 2.0 copy-start.3
  1100.8 1.7 copy-start.1
  1125.9 131.7 %all-to-all-start.1 = ((bf16[8,64,4096]{2,1,0:T(8,128)(2,1)}), bf16[8,64,4096]{2,1,0:T(8,128)(2,1)}, u32[]{:S(2)}, u32[]{:S(2)}) async-start(bf16[8,64,4096]{2,1,0:T(8,128)(2,1)} %bitcast.44), calls=%async_computation.1 | async-start | bytes 8388608 | tf_op jit(solution)/shard_map/all_to_all | solution.py:137
  1132.6 360.8 %all-reduce.4.cloned.1.call-start = ((), (), s32[]{:S(2)}) async-start(), calls=%async_computation.2 | async-start | bytes 262144 | tf_op jit(solution)/shard_map/psum | solution.py:138
  1493.4 4.7 copy-start.7
Sparse Core Ops, SparseCore 0:
  95.4 681.5 all-gather.2
  793.3 304.4 all-reduce.5
  1254.1 239.3 all-reduce.3
where the time goes:
time: 1510 us
  waiting for transfers between devices  1260 us (83%)
  blocking collectives  112 us (7%)
  local copies, waits for them, and re-layouts  54.7 us (4%)
  other arithmetic  27.5 us (2%)
  matrix products  17.5 us (1%)
  between operations  16.5 us (1%)
    all_gather x1, waiting for transfers between devices, shards(): records_all = lax.all_gather(records, ('dp', 'expert'), axis=0, tiled=True)  681 us
    unnamed x4, waiting for transfers between devices  301 us
    psum x1, waiting for transfers between devices, shards(): lax.psum((router_part, loss_local), ('dp', 'expert'))  236 us
    psum x1, blocking collectives, shards(): lax.psum((router_part, loss_local), ('dp', 'expert'))  112 us
    all_to_all x1, waiting for transfers between devices, shards(): lax.all_to_all(expert_out.reshape(experts, capacity, hidden_width), 'expe...  45.7 us
  transfers between devices with their start and end apart: 5, of which 4 were waited for; matrix products, arithmetic and copies ran while one was open for 1% of the time, Pallas kernels for 0%

commit v1 on v0

--- a/solution.py
+++ b/solution.py
@@ -135,7 +135,7 @@
         tokens, router, norm_gain, saved, grad_pool, experts, capacity
     )
     returned = lax.all_to_all(sendback, "expert", split_axis=0, concat_axis=0, tiled=True)
-    router_grad, loss_total = lax.psum((router_part, loss_local), ("dp", "expert"))
+    router_grad, loss_total = lax.psum(lax.psum((router_part, loss_local), "dp"), "expert")
     expert_grad = returned.reshape(1, 1, experts, capacity, hidden_width)
     return (token_grad, expert_grad, router_grad, loss_total / pair_total)
 

time: 1510 us -> 1440 us (0.954)
  blocking collectives: 112 us -> 78.1 us
  waiting for transfers between devices: 1260 us -> 1230 us
    psum x1 -> x2, blocking collectives: 112 us -> 78.1 us  [the longest x1 56.6 us: shards(): lax.psum((router_part, loss_local), 'dp')]
    psum x1 -> x2, waiting for transfers between devices: 236 us -> 203 us  [the longest x1 120 us: shards(): lax.psum((router_part, loss_local), 'dp')]
    unnamed x4 -> x5, waiting for transfers between devices: 301 us -> 301 us
  transfers between devices with their start and end apart: 5 -> 6, of which waited for: 4 -> 5; matrix products, arithmetic and copies ran while one was open for 1% -> 1% of each run, Pallas kernels for 0% -> 0%
where the time goes in v1:
time: 1440 us
  waiting for transfers between devices  1230 us (85%)
  blocking collectives  78.1 us (5%)
  local copies, waits for them, and re-layouts  54.7 us (4%)
  other arithmetic  27.5 us (2%)
  matrix products  17.5 us (1%)
  between operations  16.5 us (1%)
  starting transfers between devices  14.6 us (1%)
    all_gather x1, waiting for transfers between devices, shards(): records_all = lax.all_gather(records, ('dp', 'expert'), axis=0, tiled=True)  681 us
    unnamed x5, waiting for transfers between devices  301 us
    psum x1, waiting for transfers between devices, shards(): lax.psum((router_part, loss_local), 'dp')  120 us
    psum x1, waiting for transfers between devices, shards(): lax.psum(lax.psum((router_part, loss_local), 'dp'), 'expert')  83 us
    psum x1, blocking collectives, shards(): lax.psum((router_part, loss_local), 'dp')  56.6 us
    all_to_all x1, waiting for transfers between devices, shards(): lax.all_to_all(expert_out.reshape(experts, capacity, hidden_width), 'expe...  45.7 us
  transfers between devices with their start and end apart: 6, of which 5 were waited for; matrix products, arithmetic and copies ran while one was open for 1% of the time, Pallas kernels for 0%

profile of v1, /device:TPU:8, one launch (start us, length us, event | category | flops | bytes accessed | tf_op | source)
XLA Modules:
  0.0 1439.9 jit_solution(11954634948594039915)
XLA Ops:
  7.2 7.5 all-to-all-start
  14.9 0.1 eq.59
  15.0 0.1 eq.55
  15.2 0.9 reduce-window.6
  16.0 0.2 slice_reduce_fusion
  16.4 0.1 reshape.211
  16.6 0.1 copy.48
  16.7 0.1 reshape.221
  16.9 0.5 fusion.20
  17.5 45.7 %all-to-all-done = bf16[8,64,4096]{2,1,0:T(8,128)(2,1)} async-done(((bf16[8,64,4096]{2,1,0:T(8,128)(2,1)}), bf16[8,64,4096]{2,1,0:T(8,128)(2,1)}, u32[]{:S(2)}, u32[]{:S(2)}) %all-to-all-start) | async-done | bytes 4194336 | tf_op jit(solution)/shard_map/all_to_all | solution.py:101
  63.2 11.0 gather_fusion
  74.2 4.6 reshape.220
  78.8 7.0 fusion.17
  85.8 4.0 multiply_reduce_fusion.2
  89.9 2.4 multiply_multiply_fusion
  92.3 0.2 copy-done.2
  92.5 2.2 reduce_sum.112
  94.7 0.6 slice_bitcast_fusion
  95.3 0.2 all-reduce.9.cloned.1.call-start
  96.2 680.8 %all-gather.3.cloned.1.call-done = bf16[256,2,4096]{2,1,0:T(2,128)(2,1)} async-done(((bf16[1,2,4096]{2,1,0:T(2,128)(2,1)}), bf16[256,2,4096]{2,1,0:T(2,128)(2,1)}) %all-gather.3.cloned.1.call-update) | async-done | bytes 4194320 | tf_op jit(solution)/shard_map/all_gather | solution.py:116
  777.0 7.2 reshape.238
  784.2 3.5 fusion.19
  787.7 0.2 select_reduce_fusion.2
  787.9 0.6 subtract_reduce_fusion
  788.5 4.6 convolution_multiply_fusion
  793.3 0.1 div.48
  793.5 0.1 reshape.214
  793.7 2.9 convolution_multiply_fusion.1
  796.6 301.1 %all-reduce.9.cloned.1.call-done = f32[512,4096]{1,0:T(8,128)} async-done(((f32[512,4096]{1,0:T(8,128)}), f32[512,4096]{1,0:T(8,128)}) %all-reduce.9.cloned.1.call-update) | async-done | bytes 8388624
  1097.7 1.1 constant_dynamic-slice_fusion
  1098.8 0.3 bitcast_multiply_fusion
  1099.2 0.5 copy-done.3
  1099.7 0.4 multiply_reduce_fusion.1
  1100.1 0.7 multiply_subtract_fusion
  1100.8 1.7 copy-done.1
  1102.5 5.3 mul.182
  1107.8 8.4 mul.189
  1116.2 9.7 scatter_custom_fusion
  1125.9 6.8 all-to-all-start.1
  1132.6 5.7 multiply_reduce_fusion
  1138.5 2.4 convolution_bitcast_fusion
  1141.0 56.6 %psum.30 = f32[]{:T(128)} all-reduce(f32[]{:T(128)} %get-tuple-element.6), channel_id=1, replica_groups=mesh['dp'=32,'expert'=8] {'dp'}, use_global_device_ids=true, to_apply=%region_20.21 | all-reduce | flops 1 | bytes 8 | tf_op jit(solution)/shard_map/psum | solution.py:138
  1197.5 21.5 %psum.31 = f32[]{:T(128)} all-reduce(f32[]{:T(128)} %psum.30), channel_id=1, replica_groups=mesh['dp'=32,'expert'=8] {'expert'}, use_global_device_ids=true, to_apply=%region_21.22 | all-reduce | flops 1 | bytes 8 | tf_op jit(solution)/shard_map/psum | solution.py:138
  1219.7 120.5 %all-reduce.5.cloned.1.call-done = f32[4096,8]{0,1:T(8,128)} async-done(((f32[4096,8]{0,1:T(8,128)}), f32[4096,8]{0,1:T(8,128)}) %all-reduce.5.cloned.1.call-update) | async-done | bytes 131088 | tf_op jit(solution)/shard_map/psum | solution.py:138
  1340.2 3.6 fusion
  1343.9 83.0 %all-reduce.7.cloned.1.call-done = f32[4096,8]{0,1:T(8,128)} async-done(((f32[4096,8]{0,1:T(8,128)}), f32[4096,8]{0,1:T(8,128)}) %all-reduce.7.cloned.1.call-update) | async-done | bytes 131088 | tf_op jit(solution)/shard_map/psum | solution.py:138
  1426.8 4.7 copy.70
  1431.6 0.7 copy.71
  (48 shorter events, 1.0 us)
Async XLA Ops:
  7.2 9.7 copy-start
  7.2 7.5 copy-start.8
  7.2 9.7 copy-start.4
  7.2 56.0 %all-to-all-start = ((bf16[8,64,4096]{2,1,0:T(8,128)(2,1)}), bf16[8,64,4096]{2,1,0:T(8,128)(2,1)}, u32[]{:S(2)}, u32[]{:S(2)}) async-start(bf16[8,64,4096]{2,1,0:T(8,128)(2,1)} %bitcast.46), calls=%async_computation | async-start | bytes 8388608 | tf_op jit(solution)/shard_map/all_to_all | solution.py:101
  14.7 762.3 %all-gather.3.cloned.1.call-start = ((), (), s32[]{:S(2)}) async-start(), calls=%async_computation.4 | async-start | bytes 4210688 | tf_op jit(solution)/shard_map/all_gather | solution.py:116
  78.8 7.0 copy-start.5
  85.8 4.1 copy-start.6
  89.8 2.6 copy-start.2
  95.3 1002.4 %all-reduce.9.cloned.1.call-start = ((), (), s32[]{:S(2)}) async-start(), calls=%async_computation.5 | async-start | bytes 16777216
  784.2 3.5 copy-start.9
  1097.7 2.0 copy-start.3
  1100.8 1.7 copy-start.1
  1125.9 218.0 %all-to-all-start.1 = ((bf16[8,64,4096]{2,1,0:T(8,128)(2,1)}), bf16[8,64,4096]{2,1,0:T(8,128)(2,1)}, u32[]{:S(2)}, u32[]{:S(2)}) async-start(bf16[8,64,4096]{2,1,0:T(8,128)(2,1)} %bitcast.44), calls=%async_computation.1 | async-start | bytes 8388608 | tf_op jit(solution)/shard_map/all_to_all | solution.py:137
  1132.6 207.5 %all-reduce.5.cloned.1.call-start = ((), (), s32[]{:S(2)}) async-start(), calls=%async_computation.2 | async-start | bytes 262144 | tf_op jit(solution)/shard_map/psum | solution.py:138
  1140.9 285.9 %all-reduce.7.cloned.1.call-start = ((), (), s32[]{:S(2)}) async-start(), calls=%async_computation.3 | async-start | bytes 262144 | tf_op jit(solution)/shard_map/psum | solution.py:138
  1426.8 4.7 copy-start.7
Sparse Core Ops, SparseCore 0:
  95.4 681.5 all-gather.2
  793.3 304.4 all-reduce.8
  1141.0 199.0 all-reduce.4
  1342.6 84.1 all-reduce.6
